TPU v7x, 256 devices: a whole 4x4x8 slice. The times are simulated.
256 devices in a mesh: row: 8 (over x, y_lo), col: 32 (over y_hi, z, core).
Axes of the slice: x: 4, y: 4 (y_hi: 2, y_lo: 2; y = y_hi * 2 + y_lo), z: 8, core: 2. Of those that a mesh axis runs over, the one named last changes fastest.
Arguments:
- features: bfloat16 [32768, 512], P(('col', 'row')), may hold values from -6 to 6
- tile_vals: bfloat16 [8, 4096, 128, 128], P('row', 'col')
- tile_row: int32 [8, 4096], P('row', 'col'), may hold values from 0 to 31
- tile_col: int32 [8, 4096], P('row', 'col'), may hold values from 0 to 7
- tile_count: int32 [8, 32], P('row', 'col'), may hold values from 1 to 128, as said below
- node_type: int32 [32768], P(('row', 'col')), may hold values from 0 to 7
- type_gain: float32 [8, 512], replicated, may hold values from 0.1 to 1.9
- w_in: bfloat16 [512, 1024], replicated, may hold values from -0.25 to 0.25
- w_out: bfloat16 [1024, 512], replicated, may hold values from -0.1875 to 0.1875
- cotangent: bfloat16 [32768, 512], P(('row', 'col')), may hold values from -6 to 6
Outputs:
- mixed: bfloat16 [32768, 512], P(('row', 'col'))
- grad_x: float32 [32768, 512], P(('col', 'row'))
- grad_w_in: float32 [512, 1024], replicated
- grad_w_out: float32 [1024, 512], replicated
- grad_gain: float32 [8, 512], replicated
Inputs may be any that keep to these rules, and one draw needn't show every extreme that they name: Slots 0 to tile_count - 1 of a grid cell's list are live; some grid cell has all 128 slots live in every draw.
All inputs are finite; a program needn't handle non-finite values.
Results may differ from a plain program's by a relative error of at most 0.0056.
Values may be sent and summed in bfloat16 or wider, within the bound.
A program may use at most 128 MiB of HBM per device.

v0:
```python
import jax
import jax.numpy as jnp
from jax import lax
from jax.sharding import PartitionSpec as P

F = 512
TYPES = 8
TILE = 128


def sweep(weights_all, row_ids_all, col_ids_all, live_count, sources, target, forward, lower):
    span = target.shape[0]
    rounds = weights_all.shape[0] // 16

    def advance(block_index, totals):
        first_slot = block_index * 16
        weights_now = lax.dynamic_slice_in_dim(weights_all, first_slot, 16, 0)
        row_ids = lax.dynamic_slice_in_dim(row_ids_all, first_slot, 16, 0)
        col_ids = lax.dynamic_slice_in_dim(col_ids_all, first_slot, 16, 0)
        living = first_slot + jnp.arange(16, dtype=jnp.int32) < live_count
        if forward:
            pieces = sources[col_ids]
            product = jnp.einsum(
                "sab,sbf->saf", weights_now, pieces, preferred_element_type=jnp.float32
            )
            destination = row_ids - lower
        else:
            pieces = sources[row_ids]
            product = jnp.einsum(
                "sab,saf->sbf", weights_now, pieces, preferred_element_type=jnp.float32
            )
            destination = col_ids - lower
        inside = living & (destination >= 0) & (destination < span)
        product = jnp.where(inside[:, None, None], product, 0.0)
        placed = jnp.clip(destination, 0, span - 1)
        return totals.at[placed].add(product)

    return lax.fori_loop(0, rounds, advance, target)


def shards(
    features,
    tile_vals,
    tile_row,
    tile_col,
    tile_count,
    node_type,
    type_gain,
    w_in,
    w_out,
    cotangent,
):
    row_count = lax.axis_size("row")
    col_count = lax.axis_size("col")
    total_nodes = TILE * row_count * col_count
    weights_all = tile_vals[0]
    row_ids_all = tile_row[0]
    col_ids_all = tile_col[0]
    live_count = tile_count[0, 0]
    gathered = lax.all_gather(features, "row", axis=0, tiled=True).reshape(row_count, TILE, F)
    totals = sweep(
        weights_all,
        row_ids_all,
        col_ids_all,
        live_count,
        gathered,
        jnp.zeros((col_count, TILE, F), jnp.float32),
        True,
        0,
    )
    aggregate = lax.psum_scatter(
        totals.reshape(col_count * TILE, F), "col", scatter_dimension=0, tiled=True
    )
    center = jnp.mean(aggregate, axis=-1, keepdims=True)
    spread = jnp.mean(jnp.square(aggregate - center), axis=-1, keepdims=True)
    inverse = lax.rsqrt(spread + 1e-05)
    normed = (aggregate - center) * inverse
    onehot = (node_type[:, None] == jnp.arange(TYPES, dtype=jnp.int32)[None, :]).astype(jnp.float32)
    gains = jnp.dot(onehot, type_gain, precision=lax.Precision.HIGHEST)
    scaled = (normed * gains).astype(jnp.bfloat16)
    hidden = jnp.dot(scaled, w_in, preferred_element_type=jnp.float32)
    activated = jax.nn.silu(hidden).astype(jnp.bfloat16)
    branch = jnp.dot(activated, w_out, preferred_element_type=jnp.float32)
    mixed = (aggregate + branch).astype(jnp.bfloat16)
    upstream = cotangent.astype(jnp.float32)
    grad_out_w = jnp.dot(activated.T, cotangent, preferred_element_type=jnp.float32)
    grad_act = jnp.dot(cotangent, w_out.T, preferred_element_type=jnp.float32)
    sigmoid_h = jax.nn.sigmoid(hidden)
    grad_hidden = (grad_act * sigmoid_h * (1.0 + hidden * (1.0 - sigmoid_h))).astype(jnp.bfloat16)
    grad_in_w = jnp.dot(scaled.T, grad_hidden, preferred_element_type=jnp.float32)
    grad_scaled = jnp.dot(grad_hidden, w_in.T, preferred_element_type=jnp.float32)
    grad_gain = jnp.dot(onehot.T, grad_scaled * normed, precision=lax.Precision.HIGHEST)
    grad_normed = grad_scaled * gains
    grad_agg = upstream + inverse * (
        grad_normed
        - jnp.mean(grad_normed, axis=-1, keepdims=True)
        - normed * jnp.mean(grad_normed * normed, axis=-1, keepdims=True)
    )
    grad_rows = grad_agg.astype(jnp.bfloat16)
    reduced = lax.psum((grad_in_w, grad_out_w, grad_gain), ("row", "col"))
    grad_sources = lax.all_gather(grad_rows, "col", axis=0, tiled=True).reshape(col_count, TILE, F)
    back = sweep(
        weights_all,
        row_ids_all,
        col_ids_all,
        live_count,
        grad_sources,
        jnp.zeros((row_count, TILE, F), jnp.float32),
        False,
        0,
    )
    grad_x = lax.psum_scatter(
        back.reshape(row_count * TILE, F), "row", scatter_dimension=0, tiled=True
    )
    factor = float(total_nodes) ** (-0.5)
    return (mixed, grad_x, reduced[0] * factor, reduced[1] * factor, reduced[2] * factor)


def solution(mesh):
    return jax.shard_map(
        shards,
        mesh=mesh,
        in_specs=(
            P(("col", "row"), None),
            P("row", "col", None, None),
            P("row", "col"),
            P("row", "col"),
            P("row", "col"),
            P(("row", "col")),
            P(),
            P(),
            P(),
            P(("row", "col"), None),
        ),
        out_specs=(P(("row", "col"), None), P(("col", "row"), None), P(), P(), P()),
        check_vma=False,
    )
```

profile of v0, /device:TPU:32, one launch (start us, length us, event | category | flops | bytes accessed | tf_op | source)
XLA Modules:
  0.0 769.9 jit_solution(11946579066212321571)
XLA Ops:
  8.0 45.8 %all-gather.3.cloned.1.call-done = bf16[1024,512]{1,0:T(8,128)(2,1)} async-done(((bf16[128,512]{1,0:T(8,128)(2,1)}), bf16[1024,512]{1,0:T(8,128)(2,1)}) %all-gather.3.cloned.1.call-update) | async-done | bytes 1048592 | tf_op jit(solution)/shard_map/all_gather | solution.py:60
  58.1 127.6 %while.26 = (s32[]{:T(128)}, f32[32,128,512]{2,1,0:T(8,128)}, s32[128]{0:T(128)S(1)}, s32[]{:T(128)}, bf16[128,128,128]{2,1,0:T(8,128)(2,1)}, /*index=5*/s32[128...) while((s32[]{:T(128)}, f32[32,128,512]{2,1,0:T(8,128)}, ...), condition=%wide.region_2.3_spmd, body=%wide.region_0.2_spmd.sunk | while | flops 270533856 | bytes 23597776 | solution.py:38
  64.5 9.6 %scatter_fusion = f32[32,128,512]{2,1,0:T(8,128)} fusion(f32[32,128,512]{2,1,0:T(8,128)} %get-tuple-element.410, s32[16]{0:T(128)S(1)} %get-tuple-element.387, f32[16,128,512]{2,1,0:T(8,128)} %convolution_select_fusion.4), kind=kCustom, calls=%fused_computation.2.clone.1 | custom fusion | flops 1048576 | bytes 12582976 | tf_op jit(solution)/shard_map/while/body/eval_jaxpr/scatter-add | solution.py:36
  80.5 9.6 %scatter_fusion = f32[32,128,512]{2,1,0:T(8,128)} fusion(f32[32,128,512]{2,1,0:T(8,128)} %get-tuple-element.410, s32[16]{0:T(128)S(1)} %get-tuple-element.387, f32[16,128,512]{2,1,0:T(8,128)} %convolution_select_fusion.4), kind=kCustom, calls=%fused_computation.2.clone.1 | custom fusion | flops 1048576 | bytes 12582976 | tf_op jit(solution)/shard_map/while/body/eval_jaxpr/scatter-add | solution.py:36
  96.5 9.5 %scatter_fusion = f32[32,128,512]{2,1,0:T(8,128)} fusion(f32[32,128,512]{2,1,0:T(8,128)} %get-tuple-element.410, s32[16]{0:T(128)S(1)} %get-tuple-element.387, f32[16,128,512]{2,1,0:T(8,128)} %convolution_select_fusion.4), kind=kCustom, calls=%fused_computation.2.clone.1 | custom fusion | flops 1048576 | bytes 12582976 | tf_op jit(solution)/shard_map/while/body/eval_jaxpr/scatter-add | solution.py:36
  112.3 9.5 %scatter_fusion = f32[32,128,512]{2,1,0:T(8,128)} fusion(f32[32,128,512]{2,1,0:T(8,128)} %get-tuple-element.410, s32[16]{0:T(128)S(1)} %get-tuple-element.387, f32[16,128,512]{2,1,0:T(8,128)} %convolution_select_fusion.4), kind=kCustom, calls=%fused_computation.2.clone.1 | custom fusion | flops 1048576 | bytes 12582976 | tf_op jit(solution)/shard_map/while/body/eval_jaxpr/scatter-add | solution.py:36
  128.2 9.7 %scatter_fusion = f32[32,128,512]{2,1,0:T(8,128)} fusion(f32[32,128,512]{2,1,0:T(8,128)} %get-tuple-element.410, s32[16]{0:T(128)S(1)} %get-tuple-element.387, f32[16,128,512]{2,1,0:T(8,128)} %convolution_select_fusion.4), kind=kCustom, calls=%fused_computation.2.clone.1 | custom fusion | flops 1048576 | bytes 12582976 | tf_op jit(solution)/shard_map/while/body/eval_jaxpr/scatter-add | solution.py:36
  144.4 9.5 %scatter_fusion = f32[32,128,512]{2,1,0:T(8,128)} fusion(f32[32,128,512]{2,1,0:T(8,128)} %get-tuple-element.410, s32[16]{0:T(128)S(1)} %get-tuple-element.387, f32[16,128,512]{2,1,0:T(8,128)} %convolution_select_fusion.4), kind=kCustom, calls=%fused_computation.2.clone.1 | custom fusion | flops 1048576 | bytes 12582976 | tf_op jit(solution)/shard_map/while/body/eval_jaxpr/scatter-add | solution.py:36
  160.3 9.4 %scatter_fusion = f32[32,128,512]{2,1,0:T(8,128)} fusion(f32[32,128,512]{2,1,0:T(8,128)} %get-tuple-element.410, s32[16]{0:T(128)S(1)} %get-tuple-element.387, f32[16,128,512]{2,1,0:T(8,128)} %convolution_select_fusion.4), kind=kCustom, calls=%fused_computation.2.clone.1 | custom fusion | flops 1048576 | bytes 12582976 | tf_op jit(solution)/shard_map/while/body/eval_jaxpr/scatter-add | solution.py:36
  176.1 9.5 %scatter_fusion = f32[32,128,512]{2,1,0:T(8,128)} fusion(f32[32,128,512]{2,1,0:T(8,128)} %get-tuple-element.410, s32[16]{0:T(128)S(1)} %get-tuple-element.387, f32[16,128,512]{2,1,0:T(8,128)} %convolution_select_fusion.4), kind=kCustom, calls=%fused_computation.2.clone.1 | custom fusion | flops 1048576 | bytes 12582976 | tf_op jit(solution)/shard_map/while/body/eval_jaxpr/scatter-add | solution.py:36
  185.7 153.5 %reduce-scatter.3.cloned.1.call-done = f32[128,512]{1,0:T(8,128)} async-done(((f32[4096,512]{1,0:T(8,128)}), f32[128,512]{1,0:T(8,128)}) %reduce-scatter.3.cloned.1.call-update) | async-done | bytes 262160 | tf_op jit(solution)/shard_map/reduce_scatter | solution.py:71
  347.1 6.4 copy.15
  357.2 75.2 %all-gather.5.cloned.1.call-done = bf16[4096,512]{1,0:T(8,128)(2,1)} async-done(((bf16[128,512]{1,0:T(8,128)(2,1)}), bf16[4096,512]{1,0:T(8,128)(2,1)}) %all-gather.5.cloned.1.call-update) | async-done | bytes 4194320 | tf_op jit(solution)/shard_map/all_gather | solution.py:101
  432.7 125.2 %while.27 = (s32[]{:T(128)}, f32[8,128,512]{2,1,0:T(8,128)S(1)}, s32[128]{0:T(128)S(1)}, s32[]{:T(128)}, bf16[128,128,128]{1,2,0:T(8,128)(2,1)}, /*index=5*/s32[...) while((s32[]{:T(128)}, f32[8,128,512]{2,1,0:T(8,128)S(1)}, ...), condition=%wide.region_10.11_spmd, body=%wide.region_8.10_spmd.sunk | while | flops 270533856 | bytes 23597776 | solution.py:38
  442.1 6.4 scatter_fusion.1
  458.0 6.1 scatter_fusion.1
  473.6 6.2 scatter_fusion.1
  489.3 6.2 scatter_fusion.1
  504.9 6.2 scatter_fusion.1
  520.5 6.2 scatter_fusion.1
  551.8 6.1 scatter_fusion.1
  560.6 75.6 %psum.23 = f32[8,512]{1,0:T(8,128)S(1)} all-reduce(f32[8,512]{1,0:T(8,128)S(1)} %fusion.7), channel_id=1, replica_groups=mesh['row'=8,'col'=32] {'row','col'}, use_global_device_ids=true, to_apply=%region_14.15 | all-reduce | flops 4096 | bytes 32768 | tf_op jit(solution)/shard_map/psum | solution.py:100
  639.2 65.0 %all-reduce.3.cloned.1.call-done = (f32[512,1024]{1,0:T(8,128)}, f32[1024,512]{1,0:T(8,128)}) async-done(((f32[512,1024]{1,0:T(8,128)}, f32[1024,512]{1,0:T(8,128)}), (f32[512,1024]{1,0:T(8,128)}, f32[1024,512]{1,0:T(8,128)})) %all-reduce.3.cloned.1.call-update) | async-done | bytes 4194320 | tf_op jit(solution)/shard_map/psum | solution.py:100
  709.0 54.3 %reduce-scatter.5.cloned.1.call-done = f32[128,512]{1,0:T(8,128)} async-done(((f32[1024,512]{1,0:T(8,128)}), f32[128,512]{1,0:T(8,128)}) %reduce-scatter.5.cloned.1.call-update) | async-done | bytes 262160 | tf_op jit(solution)/shard_map/reduce_scatter | solution.py:112
  (130 shorter events, 160.0 us)
Async XLA Ops:
  7.2 335.6 %copy-start = (bf16[512,1024]{1,0:T(8,128)(2,1)S(1)}, bf16[512,1024]{1,0:T(8,128)(2,1)}, u32[]{:S(2)}) copy-start(bf16[512,1024]{1,0:T(8,128)(2,1)} %param.21) | copy-start | bytes 3145732
  7.2 46.6 %all-gather.3.cloned.1.call-start = ((), (), s32[]{:S(2)}) async-start(), calls=%async_computation.2 | async-start | bytes 1179648 | tf_op jit(solution)/shard_map/all_gather | solution.py:60
  7.9 331.3 %reduce-scatter.3.cloned.1.call-start = ((), (), s32[]{:S(2)}) async-start(), calls=%async_computation.3 | async-start | bytes 8650752 | tf_op jit(solution)/shard_map/reduce_scatter | solution.py:71
  53.8 4.3 copy-start.6
  53.8 4.3 copy-start.7
  185.6 155.8 %copy-start.8 = (f32[8,512]{1,0:T(8,128)S(1)}, f32[8,512]{1,0:T(8,128)}, u32[]{:S(2)}) copy-start(f32[8,512]{1,0:T(8,128)} %param.20) | copy-start | bytes 49156
  185.6 155.8 %copy-start.9 = (s32[128]{0:T(128)S(1)}, s32[128]{0:T(128)}, u32[]{:S(2)}) copy-start(s32[128]{0:T(128)} %param.19) | copy-start | bytes 1540
  185.6 157.4 %copy-start.5 = (bf16[128,512]{1,0:T(8,128)(2,1)S(1)}, bf16[128,512]{1,0:T(8,128)(2,1)}, u32[]{:S(2)}) copy-start(bf16[128,512]{1,0:T(8,128)(2,1)} %param.23) | copy-start | bytes 393220
  185.6 246.8 %all-gather.5.cloned.1.call-start = ((), (), s32[]{:S(2)}) async-start(), calls=%async_computation.4 | async-start | bytes 4325376 | tf_op jit(solution)/shard_map/all_gather | solution.py:101
  343.1 12.3 %copy-start.4 = (f32[128,1024]{1,0:T(8,128)}, f32[128,1024]{1,0:T(8,128)S(1)}, u32[]{:S(2)}) copy-start(f32[128,1024]{1,0:T(8,128)S(1)} %fusion.16) | copy-start | bytes 1572868
  343.1 1.9 copy-start.2
  347.1 357.1 %all-reduce.3.cloned.1.call-start = ((), (), s32[]{:S(2)}) async-start(), calls=%async_computation.6 | async-start | bytes 8388608 | tf_op jit(solution)/shard_map/psum | solution.py:100
  357.2 406.2 %reduce-scatter.5.cloned.1.call-start = ((), (), s32[]{:S(2)}) async-start(), calls=%async_computation.5 | async-start | bytes 2359296 | tf_op jit(solution)/shard_map/reduce_scatter | solution.py:112
  557.9 1.3 copy-start.1
  704.2 3.3 copy-start.3
Sparse Core Ops, SparseCore 0:
  9.8 43.9 all-gather.2
  185.8 153.4 reduce-scatter.2
  347.2 85.2 all-gather.4
  438.5 265.6 all-reduce.2
  707.2 56.1 reduce-scatter.4
where the time goes:
time: 772 us; the launch traced here: 770 us
  waiting for transfers between devices  395 us (51%)
  other arithmetic  147 us (19%)
  matrix products  76.7 us (10%)
  blocking collectives  75.6 us (10%)
  local copies, waits for them, and re-layouts  61.2 us (8%)
  between operations  13.9 us (2%)
    reduce_scatter x1, waiting for transfers between devices, shards(): lax.psum_scatter(totals.reshape(col_count * TILE, F), 'col', scatter_dime...  154 us
    scatter-add x16, other arithmetic, advance(): return totals.at[placed].add(product)  126 us
    psum x1, blocking collectives, shards(): reduced = lax.psum((grad_in_w, grad_out_w, grad_gain), ('row', 'col'))  75.6 us
    all_gather x1, waiting for transfers between devices, shards(): lax.all_gather(grad_rows, 'col', axis=0, tiled=True)  75.2 us
    psum x1, waiting for transfers between devices, shards(): reduced = lax.psum((grad_in_w, grad_out_w, grad_gain), ('row', 'col'))  65 us
    reduce_scatter x1, waiting for transfers between devices, shards(): lax.psum_scatter(back.reshape(row_count * TILE, F), 'row', scatter_dimens...  54.3 us
    all_gather x1, waiting for transfers between devices, shards(): lax.all_gather(features, 'row', axis=0, tiled=True)  45.8 us
    dot_general x8, matrix products, advance(): jnp.einsum('sab,saf->sbf', weights_now, pieces, preferred_element_type=jn...  35.3 us
  transfers between devices with their start and end apart: 5, of which 5 were waited for; matrix products, arithmetic and copies ran while one was open for 19% of the time, Pallas kernels for 0%

commit v1 on v0

--- a/solution.py
+++ b/solution.py
@@ -98,7 +98,9 @@
     )
     grad_rows = grad_agg.astype(jnp.bfloat16)
     reduced = lax.psum((grad_in_w, grad_out_w, grad_gain), ("row", "col"))
-    grad_sources = lax.all_gather(grad_rows, "col", axis=0, tiled=True).reshape(col_count, TILE, F)
+    grad_sources = jnp.concatenate(
+        lax.all_to_all(jnp.stack([grad_rows] * lax.axis_size("col")), "col", 0, 0), axis=0
+    ).reshape(col_count, TILE, F)
     back = sweep(
         weights_all,
         row_ids_all,

time: 772 us -> 736 us (0.953)
  waiting for transfers between devices: 395 us -> 347 us
    all_to_all x0 -> x1, waiting for transfers between devices: none -> 94.6 us  [shards(): lax.all_to_all(jnp.stack([grad_rows] * lax.axis_size('col')), 'col', 0, 0)]
    all_gather x1 -> x0, waiting for transfers between devices: 75.2 us -> none  [shards(): lax.all_gather(grad_rows, 'col', axis=0, tiled=True)]
    psum x1, waiting for transfers between devices: 65 us -> 0.01 us  [shards(): reduced = lax.psum((grad_in_w, grad_out_w, grad_gain), ('row', 'col'))]
  transfers between devices with their start and end apart: 5 -> 5, of which waited for: 5 -> 4; matrix products, arithmetic and copies ran while one was open for 19% -> 20% of each run, Pallas kernels for 0% -> 0%
where the time goes in v1:
time: 736 us; the launch traced here: 734 us
  waiting for transfers between devices  347 us (47%)
  other arithmetic  146 us (20%)
  blocking collectives  78.6 us (11%)
  matrix products  76.7 us (10%)
  local copies, waits for them, and re-layouts  63.6 us (9%)
  between operations  13.9 us (2%)
    reduce_scatter x1, waiting for transfers between devices, shards(): lax.psum_scatter(totals.reshape(col_count * TILE, F), 'col', scatter_dime...  154 us
    scatter-add x16, other arithmetic, advance(): return totals.at[placed].add(product)  125 us
    all_to_all x1, waiting for transfers between devices, shards(): lax.all_to_all(jnp.stack([grad_rows] * lax.axis_size('col')), 'col', 0, 0)  94.6 us
    psum x1, blocking collectives, shards(): reduced = lax.psum((grad_in_w, grad_out_w, grad_gain), ('row', 'col'))  78.6 us
    reduce_scatter x1, waiting for transfers between devices, shards(): lax.psum_scatter(back.reshape(row_count * TILE, F), 'row', scatter_dimens...  52.2 us
    all_gather x1, waiting for transfers between devices, shards(): lax.all_gather(features, 'row', axis=0, tiled=True)  45.8 us
    dot_general x8, matrix products, advance(): jnp.einsum('sab,saf->sbf', weights_now, pieces, preferred_element_type=jn...  35.3 us
    gather x8, local copies, waits for them, and re-layouts, advance(): pieces = sources[row_ids]  33.6 us
  transfers between devices with their start and end apart: 5, of which 4 were waited for; matrix products, arithmetic and copies ran while one was open for 20% of the time, Pallas kernels for 0%

profile of v1, /device:TPU:32, one launch (start us, length us, event | category | flops | bytes accessed | tf_op | source)
XLA Modules:
  0.0 733.6 jit_solution(11256846463107069367)
XLA Ops:
  8.0 45.8 %all-gather.2.cloned.1.call-done = bf16[1024,512]{1,0:T(8,128)(2,1)} async-done(((bf16[128,512]{1,0:T(8,128)(2,1)}), bf16[1024,512]{1,0:T(8,128)(2,1)}) %all-gather.2.cloned.1.call-update) | async-done | bytes 1048592 | tf_op jit(solution)/shard_map/all_gather | solution.py:60
  58.1 127.5 %while.26 = (s32[]{:T(128)}, f32[32,128,512]{2,1,0:T(8,128)}, s32[128]{0:T(128)S(1)}, s32[]{:T(128)}, bf16[128,128,128]{2,1,0:T(8,128)(2,1)}, /*index=5*/s32[128...) while((s32[]{:T(128)}, f32[32,128,512]{2,1,0:T(8,128)}, ...), condition=%wide.region_2.3_spmd, body=%wide.region_0.2_spmd.sunk | while | flops 270533856 | bytes 23597776 | solution.py:38
  64.5 9.6 %scatter_fusion = f32[32,128,512]{2,1,0:T(8,128)} fusion(f32[32,128,512]{2,1,0:T(8,128)} %get-tuple-element.410, s32[16]{0:T(128)S(1)} %get-tuple-element.387, f32[16,128,512]{2,1,0:T(8,128)} %convolution_select_fusion.4), kind=kCustom, calls=%fused_computation.2.clone.1 | custom fusion | flops 1048576 | bytes 12582976 | tf_op jit(solution)/shard_map/while/body/eval_jaxpr/scatter-add | solution.py:36
  80.5 9.5 %scatter_fusion = f32[32,128,512]{2,1,0:T(8,128)} fusion(f32[32,128,512]{2,1,0:T(8,128)} %get-tuple-element.410, s32[16]{0:T(128)S(1)} %get-tuple-element.387, f32[16,128,512]{2,1,0:T(8,128)} %convolution_select_fusion.4), kind=kCustom, calls=%fused_computation.2.clone.1 | custom fusion | flops 1048576 | bytes 12582976 | tf_op jit(solution)/shard_map/while/body/eval_jaxpr/scatter-add | solution.py:36
  96.4 9.4 %scatter_fusion = f32[32,128,512]{2,1,0:T(8,128)} fusion(f32[32,128,512]{2,1,0:T(8,128)} %get-tuple-element.410, s32[16]{0:T(128)S(1)} %get-tuple-element.387, f32[16,128,512]{2,1,0:T(8,128)} %convolution_select_fusion.4), kind=kCustom, calls=%fused_computation.2.clone.1 | custom fusion | flops 1048576 | bytes 12582976 | tf_op jit(solution)/shard_map/while/body/eval_jaxpr/scatter-add | solution.py:36
  112.3 9.5 %scatter_fusion = f32[32,128,512]{2,1,0:T(8,128)} fusion(f32[32,128,512]{2,1,0:T(8,128)} %get-tuple-element.410, s32[16]{0:T(128)S(1)} %get-tuple-element.387, f32[16,128,512]{2,1,0:T(8,128)} %convolution_select_fusion.4), kind=kCustom, calls=%fused_computation.2.clone.1 | custom fusion | flops 1048576 | bytes 12582976 | tf_op jit(solution)/shard_map/while/body/eval_jaxpr/scatter-add | solution.py:36
  128.2 9.7 %scatter_fusion = f32[32,128,512]{2,1,0:T(8,128)} fusion(f32[32,128,512]{2,1,0:T(8,128)} %get-tuple-element.410, s32[16]{0:T(128)S(1)} %get-tuple-element.387, f32[16,128,512]{2,1,0:T(8,128)} %convolution_select_fusion.4), kind=kCustom, calls=%fused_computation.2.clone.1 | custom fusion | flops 1048576 | bytes 12582976 | tf_op jit(solution)/shard_map/while/body/eval_jaxpr/scatter-add | solution.py:36
  144.3 9.5 %scatter_fusion = f32[32,128,512]{2,1,0:T(8,128)} fusion(f32[32,128,512]{2,1,0:T(8,128)} %get-tuple-element.410, s32[16]{0:T(128)S(1)} %get-tuple-element.387, f32[16,128,512]{2,1,0:T(8,128)} %convolution_select_fusion.4), kind=kCustom, calls=%fused_computation.2.clone.1 | custom fusion | flops 1048576 | bytes 12582976 | tf_op jit(solution)/shard_map/while/body/eval_jaxpr/scatter-add | solution.py:36
  160.2 9.4 %scatter_fusion = f32[32,128,512]{2,1,0:T(8,128)} fusion(f32[32,128,512]{2,1,0:T(8,128)} %get-tuple-element.410, s32[16]{0:T(128)S(1)} %get-tuple-element.387, f32[16,128,512]{2,1,0:T(8,128)} %convolution_select_fusion.4), kind=kCustom, calls=%fused_computation.2.clone.1 | custom fusion | flops 1048576 | bytes 12582976 | tf_op jit(solution)/shard_map/while/body/eval_jaxpr/scatter-add | solution.py:36
  176.0 9.5 %scatter_fusion = f32[32,128,512]{2,1,0:T(8,128)} fusion(f32[32,128,512]{2,1,0:T(8,128)} %get-tuple-element.410, s32[16]{0:T(128)S(1)} %get-tuple-element.387, f32[16,128,512]{2,1,0:T(8,128)} %convolution_select_fusion.4), kind=kCustom, calls=%fused_computation.2.clone.1 | custom fusion | flops 1048576 | bytes 12582976 | tf_op jit(solution)/shard_map/while/body/eval_jaxpr/scatter-add | solution.py:36
  185.6 153.8 %reduce-scatter.3.cloned.1.call-done = f32[128,512]{1,0:T(8,128)} async-done(((f32[4096,512]{1,0:T(8,128)}), f32[128,512]{1,0:T(8,128)}) %reduce-scatter.3.cloned.1.call-update) | async-done | bytes 262160 | tf_op jit(solution)/shard_map/reduce_scatter | solution.py:71
  349.0 7.0 all-to-all-start
  356.1 6.4 copy.15
  366.1 94.6 %all-to-all-done = bf16[32,128,512]{2,1,0:T(8,128)(2,1)} async-done(((bf16[32,128,512]{2,1,0:T(8,128)(2,1)}), bf16[32,128,512]{2,1,0:T(8,128)(2,1)}, u32[]{:S(2)}, u32[]{:S(2)}) %all-to-all-start) | async-done | bytes 4194336 | tf_op jit(solution)/shard_map/all_to_all | solution.py:102
  461.0 124.8 %while.27 = (s32[]{:T(128)}, f32[8,128,512]{2,1,0:T(8,128)S(1)}, s32[128]{0:T(128)S(1)}, s32[]{:T(128)}, bf16[128,128,128]{1,2,0:T(8,128)(2,1)}, /*index=5*/s32[...) while((s32[]{:T(128)}, f32[8,128,512]{2,1,0:T(8,128)S(1)}, ...), condition=%wide.region_10.11_spmd, body=%wide.region_8.10_spmd.sunk | while | flops 270533856 | bytes 23597776 | solution.py:38
  470.5 6.1 scatter_fusion.1
  501.7 6.1 scatter_fusion.1
  517.3 6.1 scatter_fusion.1
  532.9 6.1 scatter_fusion.1
  548.5 6.2 scatter_fusion.1
  564.1 6.1 scatter_fusion.1
  579.7 6.2 scatter_fusion.1
  588.5 78.6 %psum.23 = f32[8,512]{1,0:T(8,128)S(1)} all-reduce(f32[8,512]{1,0:T(8,128)S(1)} %fusion.7), channel_id=1, replica_groups=mesh['row'=8,'col'=32] {'row','col'}, use_global_device_ids=true, to_apply=%region_14.15 | all-reduce | flops 4096 | bytes 32768 | tf_op jit(solution)/shard_map/psum | solution.py:100
  674.9 52.2 %reduce-scatter.5.cloned.1.call-done = f32[128,512]{1,0:T(8,128)} async-done(((f32[1024,512]{1,0:T(8,128)}), f32[128,512]{1,0:T(8,128)}) %reduce-scatter.5.cloned.1.call-update) | async-done | bytes 262160 | tf_op jit(solution)/shard_map/reduce_scatter | solution.py:114
  (130 shorter events, 161.7 us)
Async XLA Ops:
  7.2 335.7 %copy-start = (bf16[512,1024]{1,0:T(8,128)(2,1)S(1)}, bf16[512,1024]{1,0:T(8,128)(2,1)}, u32[]{:S(2)}) copy-start(bf16[512,1024]{1,0:T(8,128)(2,1)} %param.21) | copy-start | bytes 3145732
  7.2 46.6 %all-gather.2.cloned.1.call-start = ((), (), s32[]{:S(2)}) async-start(), calls=%async_computation.3 | async-start | bytes 1179648 | tf_op jit(solution)/shard_map/all_gather | solution.py:60
  7.9 331.4 %reduce-scatter.3.cloned.1.call-start = ((), (), s32[]{:S(2)}) async-start(), calls=%async_computation.4 | async-start | bytes 8650752 | tf_op jit(solution)/shard_map/reduce_scatter | solution.py:71
  53.8 4.3 copy-start.6
  53.8 4.3 copy-start.7
  185.5 156.1 %copy-start.8 = (f32[8,512]{1,0:T(8,128)S(1)}, f32[8,512]{1,0:T(8,128)}, u32[]{:S(2)}) copy-start(f32[8,512]{1,0:T(8,128)} %param.20) | copy-start | bytes 49156
  185.5 156.1 %copy-start.9 = (s32[128]{0:T(128)S(1)}, s32[128]{0:T(128)}, u32[]{:S(2)}) copy-start(s32[128]{0:T(128)} %param.19) | copy-start | bytes 1540
  185.6 157.6 %copy-start.5 = (bf16[128,512]{1,0:T(8,128)(2,1)S(1)}, bf16[128,512]{1,0:T(8,128)(2,1)}, u32[]{:S(2)}) copy-start(bf16[128,512]{1,0:T(8,128)(2,1)} %param.23) | copy-start | bytes 393220
  343.2 21.0 %copy-start.4 = (f32[128,1024]{1,0:T(8,128)}, f32[128,1024]{1,0:T(8,128)S(1)}, u32[]{:S(2)}) copy-start(f32[128,1024]{1,0:T(8,128)S(1)} %fusion.16) | copy-start | bytes 1572868
  343.2 1.9 copy-start.2
  349.0 111.8 %all-to-all-start = ((bf16[32,128,512]{2,1,0:T(8,128)(2,1)}), bf16[32,128,512]{2,1,0:T(8,128)(2,1)}, u32[]{:S(2)}, u32[]{:S(2)}) async-start(bf16[32,128,512]{2,1,0:T(8,128)(2,1)} %stack.2), calls=%async_computation.1 | async-start | bytes 8388608 | tf_op jit(solution)/shard_map/all_to_all | solution.py:102
  356.0 314.0 %all-reduce.3.cloned.1.call-start = ((), (), s32[]{:S(2)}) async-start(), calls=%async_computation.6 | async-start | bytes 8388608 | tf_op jit(solution)/shard_map/psum | solution.py:100
  366.1 361.0 %reduce-scatter.5.cloned.1.call-start = ((), (), s32[]{:S(2)}) async-start(), calls=%async_computation.5 | async-start | bytes 2359296 | tf_op jit(solution)/shard_map/reduce_scatter | solution.py:114
  585.9 1.3 copy-start.1
  670.1 3.3 copy-start.3
Sparse Core Ops, SparseCore 0:
  9.8 43.9 all-gather.1
  185.7 153.6 reduce-scatter.2
  366.2 301.7 all-reduce.2
  671.0 56.0 reduce-scatter.4
